TPU v7x, 512 devices: a whole 4x8x8 slice. The times are simulated.
512 devices in a mesh: ctx: 32 (over y, z_lo), head: 4 (over x), batch: 4 (over z_hi, core).
Axes of the slice: x: 4, y: 8, z: 8 (z_hi: 2, z_lo: 4; z = z_hi * 4 + z_lo), core: 2. Of those that a mesh axis runs over, the one named last changes fastest.
Arguments:
- queries: bfloat16 [4, 4096, 20, 128], P('batch', 'ctx', 'head'), may hold values from -64 to 64
- key_rows: bfloat16 [4, 4096, 4, 128], P('batch', 'ctx', 'head'), may hold values from -8 to 8
- block_order: int32 [64], replicated, may hold values from 0 to 63, each once
- conv_len: int32 [4], replicated, may hold values from 2048 to 4096
- gate_wq: float32 [128, 128], replicated, may hold values from -32 to 32
- gate_wk: float32 [384, 128], replicated, may hold values from -32 to 32
Outputs:
- teacher_map: float32 [4, 20, 64, 64], P('batch', 'head', 'ctx')
- grad_wq: float32 [128, 128], replicated
- grad_wk: float32 [384, 128], replicated
All inputs are finite; a program needn't handle non-finite values.
Results may differ from a plain program's by a relative error of at most 0.0003.
Values may be sent and summed in bfloat16 or wider, within the bound.
No kernel may reach another device: no remote copies, remote signals or barrier semaphores. Data moves between devices by JAX's collectives and lax.ppermute only.
A program may use at most 64 MiB of HBM per device.

v0:
```python
import math
import jax
import jax.numpy as jnp
from jax import lax
from jax.sharding import PartitionSpec as P

BLK = 64
masked_value = -1e30
norm_epsilon = 1e-06


def score_tile(query_group, key_tile, query_pos, key_pos, length):
    scores = jnp.einsum(
        "rgqd,kgd->gqrk", query_group, key_tile, preferred_element_type=jnp.float32
    ) / math.sqrt(key_tile.shape[-1])
    allowed = (key_pos[None, :] <= query_pos[:, None]) & (key_pos[None, :] < length)
    return (jnp.where(allowed, scores, masked_value), allowed)


def gate_loss(
    weight_query, weight_key, pooled_query, pooled_key, target_map, query_starts, key_starts, length
):
    kv_heads = pooled_key.shape[1]
    group_size = pooled_query.shape[1] // kv_heads
    width_gate = weight_query.shape[1]
    proj_query = jnp.einsum(
        "bhd,de->bhe", pooled_query, weight_query, precision=lax.Precision.HIGHEST
    )
    proj_key = jnp.einsum("bgd,de->bge", pooled_key, weight_key, precision=lax.Precision.HIGHEST)
    unit_query = proj_query * lax.rsqrt(
        jnp.mean(proj_query * proj_query, axis=-1, keepdims=True) + norm_epsilon
    )
    unit_key = proj_key * lax.rsqrt(
        jnp.mean(proj_key * proj_key, axis=-1, keepdims=True) + norm_epsilon
    )
    query_count = unit_query.shape[0]
    unit_query = unit_query.reshape(query_count, kv_heads, group_size, width_gate)
    logits = jnp.einsum(
        "igqe,jge->gqij", unit_query, unit_key, precision=lax.Precision.HIGHEST
    ) / math.sqrt(width_gate)
    logits = logits.reshape(kv_heads * group_size, query_count, unit_key.shape[0])
    allowed = (key_starts[None, :] <= query_starts[:, None]) & (key_starts[None, :] < length)
    weights_exp = jnp.where(allowed[None], jnp.exp(logits), 0.0)
    log_norm = jnp.log(jnp.sum(weights_exp, axis=-1, keepdims=True))
    positive = target_map > 0
    entropy_part = jnp.where(
        positive, target_map * jnp.log(jnp.where(positive, target_map, 1.0)), 0.0
    )
    divergence = entropy_part - target_map * (logits - log_norm)
    return jnp.sum(divergence)


def body(queries, key_rows, block_order, conv_len, gate_wq, gate_wk):
    tok_dev = queries.shape[1]
    head_dev = queries.shape[2]
    kv_dev = key_rows.shape[2]
    head_size = queries.shape[3]
    group_size = head_dev // kv_dev
    block_dev = tok_dev // BLK
    block_count = block_order.shape[0]
    ctx_index = lax.axis_index("ctx")
    length = lax.dynamic_index_in_dim(conv_len, lax.axis_index("batch"), keepdims=False)
    own_blocks = lax.dynamic_slice_in_dim(block_order, ctx_index * block_dev, block_dev)
    offsets = jnp.arange(BLK, dtype=jnp.int32)
    query_pos = (own_blocks[:, None] * BLK + offsets[None, :]).reshape(tok_dev)
    valid_row = (query_pos < length)[:, None]
    query_group = queries[0].reshape(tok_dev, kv_dev, group_size, head_size)

    def tile_loop(update, carry, segment):
        width_keys = segment.shape[1]
        sub_rows = math.gcd(width_keys, 512)
        key_pos = (block_order[:, None] * BLK + offsets[None, :]).reshape(width_keys)

        def advance(step_index, state):
            first = step_index * sub_rows
            key_tile = lax.dynamic_slice_in_dim(segment[0], first, sub_rows, 0)
            tile_pos = lax.dynamic_slice_in_dim(key_pos, first, sub_rows, 0)
            column = first // BLK
            result = update(state, key_tile, tile_pos, column)
            return result

        return lax.fori_loop(0, width_keys // sub_rows, advance, carry)

    def merge_stats(highest, summed, masked, allowed):
        new_high = jnp.maximum(highest, jnp.max(masked, axis=-1))
        fresh = jnp.sum(jnp.where(allowed, jnp.exp(masked - new_high[..., None]), 0.0), axis=-1)
        return (new_high, summed * jnp.exp(highest - new_high) + fresh)

    stats_shape = (kv_dev, group_size, tok_dev)
    start_high = jnp.full(stats_shape, masked_value, jnp.float32)
    start_sum = jnp.zeros(stats_shape, jnp.float32)

    def add_stats(state, key_tile, tile_pos, column):
        masked, allowed = score_tile(query_group, key_tile, query_pos, tile_pos, length)
        return merge_stats(state[0], state[1], masked, allowed)

    highest, summed = tile_loop(
        add_stats, (start_high, start_sum), lax.all_gather(key_rows, "ctx", axis=1, tiled=True)
    )
    log_total = highest + jnp.log(summed)

    def add_pool(state, key_tile, tile_pos, column):
        masked, allowed = score_tile(query_group, key_tile, query_pos, tile_pos, length)
        probs = jnp.where(valid_row, jnp.exp(masked - log_total[..., None]), 0.0)
        tile_max = probs.reshape(
            kv_dev, group_size, block_dev, BLK, key_tile.shape[0] // BLK, BLK
        ).max(axis=(3, 5))
        return lax.dynamic_update_slice_in_dim(state, tile_max, column, 3)

    start_pool = jnp.zeros((kv_dev, group_size, block_dev, block_count), jnp.float32)
    pooled = tile_loop(add_pool, start_pool, lax.all_gather(key_rows, "ctx", axis=1, tiled=True))
    pooled = pooled.reshape(head_dev, block_dev, block_count)
    query_starts = own_blocks * BLK
    valid_block = (query_starts < length)[None, :, None]
    totals = jnp.sum(pooled, axis=-1, keepdims=True)
    target = jnp.where(valid_block, pooled / jnp.where(valid_block, totals, 1.0), 0.0)
    key_local = key_rows[0].reshape(block_dev, BLK, kv_dev, head_size)
    pooled_local = jnp.concatenate(
        [
            jnp.max(key_local, axis=1).astype(jnp.float32),
            jnp.min(key_local, axis=1).astype(jnp.float32),
            jnp.mean(key_local, axis=1, dtype=jnp.float32),
        ],
        axis=-1,
    )
    pooled_all = lax.all_gather(pooled_local, "ctx", axis=0, tiled=True)
    pooled_query = jnp.mean(
        queries[0].reshape(block_dev, BLK, head_dev, head_size), axis=1, dtype=jnp.float32
    )
    key_starts = block_order * BLK

    def local_loss(weight_query, weight_key):
        return gate_loss(
            weight_query,
            weight_key,
            pooled_query,
            pooled_all,
            target,
            query_starts,
            key_starts,
            length,
        )

    loss_value, pullback = jax.vjp(local_loss, gate_wq, gate_wk)
    grad_query, grad_key = pullback(jnp.ones((), jnp.float32))
    grad_query, grad_key = lax.psum((grad_query, grad_key), ("ctx", "head", "batch"))
    return (target[None], grad_query, grad_key)


def solution(mesh):
    in_specs = (
        P("batch", "ctx", "head", None),
        P("batch", "ctx", "head", None),
        P(),
        P(),
        P(),
        P(),
    )
    out_specs = (P("batch", "head", "ctx", None), P(), P())
    return jax.shard_map(body, mesh=mesh, in_specs=in_specs, out_specs=out_specs, check_vma=False)
```

profile of v0, /device:TPU:23, one launch (start us, length us, event | category | flops | bytes accessed | tf_op | source)
XLA Modules:
  0.0 550.4 jit_solution(3898082681139945655)
XLA Ops:
  10.4 56.8 %all_gather.8 = f32[64,1,384]{2,1,0:T(1,128)S(1)} all-gather(f32[2,1,384]{2,1,0:T(1,128)S(1)} %pad_maximum_fusion), channel_id=1, replica_groups=mesh['ctx'=32,'head'=4,'batch'=4] {'ctx'}, dimensions={0}, use_global_device_ids=true | all-gather | bytes 101376 | tf_op jit(solution)/shard_map/all_gather | solution.py:126
  67.2 1.2 dynamic_slice.35
  68.4 1.4 broadcast_compare_fusion.4
  69.8 1.0 convert_reduce_fusion
  70.8 1.3 broadcast_compare_fusion.3
  72.4 1.1 multiply_reduce_fusion.3
  74.0 63.9 %all-gather.2.cloned.1.call-done = bf16[1,4096,1,128]{3,1,2,0:T(8,128)(2,1)} async-done(((bf16[1,128,1,128]{3,1,2,0:T(8,128)(2,1)}), bf16[1,4096,1,128]{3,1,2,0:T(8,128)(2,1)}) %all-gather.2.cloned.1.call-update) | async-done | bytes 1048592 | tf_op jit(solution)/shard_map/all_gather | solution.py:111
  137.8 22.0 %while.33 = (s32[]{:T(128)}, f32[1,5,128]{2,1,0:T(8,128)S(1)}, f32[1,5,128]{2,1,0:T(8,128)S(1)}, s32[4096]{0:T(1024)S(1)}, s32[]{:T(128)}, /*index=5*/bf16[1,409...) while((s32[]{:T(128)}, f32[1,5,128]{2,1,0:T(8,128)S(1)}, ...), condition=%wide.region_3.4_spmd.clone, body=%wide.region_0.3_spmd.clone.sunk | while | flops 85987080 | bytes 3155650 | solution.py:82
  138.9 1.3 fusion.74
  141.7 1.3 fusion.74
  144.4 1.3 fusion.74
  147.2 1.3 fusion.74
  149.9 1.3 fusion.74
  152.7 1.3 fusion.74
  155.4 1.3 fusion.74
  158.2 1.3 fusion.74
  159.9 74.3 %while.34 = (s32[]{:T(128)}, f32[1,5,2,64]{3,2,1,0:T(2,128)S(1)}, s32[4096]{0:T(1024)S(1)}, s32[]{:T(128)}, bf16[1,4096,1,128]{3,1,2,0:T(8,128)(2,1)}, /*index=5...) while((s32[]{:T(128)}, f32[1,5,2,64]{3,2,1,0:T(2,128)S(1)}, ...), condition=%wide.region_6.7_spmd.clone.clone, body=%wide.region_4.6_spmd.clone.clone.sunk | while | flops 85656376 | bytes 5683170 | solution.py:82
  161.8 2.5 exponential_select_fusion.2
  164.3 2.8 reshape.363
  167.1 1.1 reduce_max.47
  170.5 2.5 exponential_select_fusion.2
  173.0 2.8 reshape.363
  175.8 1.1 reduce_max.47
  179.9 2.5 exponential_select_fusion.2
  182.4 2.8 reshape.363
  185.2 1.1 reduce_max.47
  186.5 0.9 dynamic_update_slice.13
  189.3 2.5 exponential_select_fusion.2
  191.8 2.8 reshape.363
  194.6 1.1 reduce_max.47
  198.6 2.5 exponential_select_fusion.2
  201.1 2.8 reshape.363
  204.0 1.1 reduce_max.47
  208.0 2.5 exponential_select_fusion.2
  210.5 2.8 reshape.363
  213.4 1.1 reduce_max.47
  214.6 0.9 dynamic_update_slice.13
  217.4 2.5 exponential_select_fusion.2
  219.9 2.8 reshape.363
  222.7 1.1 reduce_max.47
  226.8 2.5 exponential_select_fusion.2
  229.3 2.8 reshape.363
  232.1 1.1 reduce_max.47
  235.4 1.2 fusion.18
  236.6 0.9 convolution_bitcast_fusion
  238.2 302.2 %all-reduce.3.cloned.1.call-done = (f32[128,128]{1,0:T(8,128)}, f32[384,128]{1,0:T(8,128)}) async-done(((f32[128,128]{1,0:T(8,128)}, f32[384,128]{1,0:T(8,128)}), (f32[128,128]{1,0:T(8,128)}, f32[384,128]{1,0:T(8,128)})) %all-reduce.3.cloned.1.call-update) | async-done | bytes 262160 | tf_op jit(solution)/shard_map/psum | solution.py:146
  540.4 1.5 copy.90
  541.9 1.6 copy.91
  (162 shorter events, 37.1 us)
Async XLA Ops:
  7.2 64.9 %copy-start = (f32[384,128]{1,0:T(8,128)S(1)}, f32[384,128]{1,0:T(8,128)}, u32[]{:S(2)}) copy-start(f32[384,128]{1,0:T(8,128)} %param.15) | copy-start | bytes 589828
  7.2 130.7 %all-gather.2.cloned.1.call-start = ((), (), s32[]{:S(2)}) async-start(), calls=%async_computation | async-start | bytes 1081344 | tf_op jit(solution)/shard_map/all_gather | solution.py:111
  7.9 532.5 %all-reduce.3.cloned.1.call-start = ((), (), s32[]{:S(2)}) async-start(), calls=%async_computation.1 | async-start | bytes 524288 | tf_op jit(solution)/shard_map/psum | solution.py:146
Sparse Core Ops, SparseCore 0:
  10.1 127.7 all-gather.1
  237.7 302.7 all-reduce.2
where the time goes:
time: 552 us; the launch traced here: 550 us
  waiting for transfers between devices  367 us (66%)
  blocking collectives  56.8 us (10%)
  other arithmetic  39.2 us (7%)
  local copies, waits for them, and re-layouts  36.8 us (7%)
  matrix products  35.6 us (6%)
  between operations  14.1 us (3%)
    psum x1, waiting for transfers between devices, body(): lax.psum((grad_query, grad_key), ('ctx', 'head', 'batch'))  302 us
    all_gather x1, waiting for transfers between devices, body(): lax.all_gather(key_rows, 'ctx', axis=1, tiled=True)  63.9 us
    all_gather x1, blocking collectives, body(): pooled_all = lax.all_gather(pooled_local, 'ctx', axis=0, tiled=True)  56.8 us
    dot_general x16, matrix products, score_tile(): jnp.einsum('rgqd,kgd->gqrk', query_group, key_tile, preferred_element_typ...  30.9 us
    reshape x8, local copies, waits for them, and re-layouts, add_pool(): probs.reshape(kv_dev, group_size, block_dev, BLK, key_tile.shape[0] // BL...  22.6 us
    lt x16, other arithmetic, score_tile(): key_pos[None, :] < length  11.6 us
  transfers between devices with their start and end apart: 2, of which 2 were waited for; matrix products, arithmetic and copies ran while one was open for 2% of the time, Pallas kernels for 0%

commit v1 on v0

--- a/solution.py
+++ b/solution.py
@@ -143,7 +143,7 @@
 
     loss_value, pullback = jax.vjp(local_loss, gate_wq, gate_wk)
     grad_query, grad_key = pullback(jnp.ones((), jnp.float32))
-    grad_query, grad_key = lax.psum((grad_query, grad_key), ("ctx", "head", "batch"))
+    grad_query, grad_key = lax.psum(lax.psum((grad_query, grad_key), "ctx"), ("head", "batch"))
     return (target[None], grad_query, grad_key)
 
 

time: 552 us -> 777 us (1.41)
  the two profiles are of different devices: /device:TPU:23 before, /device:TPU:1 now
where the time goes in v1:
time: 777 us; the launch traced here: 776 us
  waiting for transfers between devices  579 us (75%)
  blocking collectives  69.9 us (9%)
  other arithmetic  39.2 us (5%)
  local copies, waits for them, and re-layouts  36.8 us (5%)
  matrix products  35.6 us (5%)
  between operations  13.9 us (2%)
    psum x1, waiting for transfers between devices, body(): lax.psum((grad_query, grad_key), 'ctx')  312 us
    psum x1, waiting for transfers between devices, body(): lax.psum(lax.psum((grad_query, grad_key), 'ctx'), ('head', 'batch'))  208 us
    all_gather x1, blocking collectives, body(): pooled_all = lax.all_gather(pooled_local, 'ctx', axis=0, tiled=True)  69.9 us
    all_gather x1, waiting for transfers between devices, body(): lax.all_gather(key_rows, 'ctx', axis=1, tiled=True)  59 us
    dot_general x16, matrix products, score_tile(): jnp.einsum('rgqd,kgd->gqrk', query_group, key_tile, preferred_element_typ...  30.9 us
    reshape x8, local copies, waits for them, and re-layouts, add_pool(): probs.reshape(kv_dev, group_size, block_dev, BLK, key_tile.shape[0] // BL...  22.6 us
  transfers between devices with their start and end apart: 3, of which 3 were waited for; matrix products, arithmetic and copies ran while one was open for 1% of the time, Pallas kernels for 0%

profile of v1, /device:TPU:1, one launch (start us, length us, event | category | flops | bytes accessed | tf_op | source)
XLA Modules:
  0.0 775.9 jit_solution(3917967442364150629)
XLA Ops:
  10.4 69.9 %all_gather.8 = f32[64,1,384]{2,1,0:T(1,128)S(1)} all-gather(f32[2,1,384]{2,1,0:T(1,128)S(1)} %pad_maximum_fusion), channel_id=1, replica_groups=mesh['ctx'=32,'head'=4,'batch'=4] {'ctx'}, dimensions={0}, use_global_device_ids=true | all-gather | bytes 101376 | tf_op jit(solution)/shard_map/all_gather | solution.py:126
  80.3 1.2 dynamic_slice.35
  81.5 1.4 broadcast_compare_fusion.4
  82.9 1.0 convert_reduce_fusion
  83.9 1.3 broadcast_compare_fusion.3
  85.6 1.1 multiply_reduce_fusion.3
  87.1 59.0 %all-gather.2.cloned.1.call-done = bf16[1,4096,1,128]{3,1,2,0:T(8,128)(2,1)} async-done(((bf16[1,128,1,128]{3,1,2,0:T(8,128)(2,1)}), bf16[1,4096,1,128]{3,1,2,0:T(8,128)(2,1)}) %all-gather.2.cloned.1.call-update) | async-done | bytes 1048592 | tf_op jit(solution)/shard_map/all_gather | solution.py:111
  146.1 22.0 %while.33 = (s32[]{:T(128)}, f32[1,5,128]{2,1,0:T(8,128)S(1)}, f32[1,5,128]{2,1,0:T(8,128)S(1)}, s32[4096]{0:T(1024)S(1)}, s32[]{:T(128)}, /*index=5*/bf16[1,409...) while((s32[]{:T(128)}, f32[1,5,128]{2,1,0:T(8,128)S(1)}, ...), condition=%wide.region_3.4_spmd.clone, body=%wide.region_0.3_spmd.clone.sunk | while | flops 85987080 | bytes 3155650 | solution.py:82
  147.2 1.3 fusion.74
  149.9 1.3 fusion.74
  152.7 1.3 fusion.74
  155.4 1.3 fusion.74
  158.2 1.3 fusion.74
  160.9 1.3 fusion.74
  163.7 1.3 fusion.74
  166.4 1.3 fusion.74
  168.1 74.3 %while.34 = (s32[]{:T(128)}, f32[1,5,2,64]{3,2,1,0:T(2,128)S(1)}, s32[4096]{0:T(1024)S(1)}, s32[]{:T(128)}, bf16[1,4096,1,128]{3,1,2,0:T(8,128)(2,1)}, /*index=5...) while((s32[]{:T(128)}, f32[1,5,2,64]{3,2,1,0:T(2,128)S(1)}, ...), condition=%wide.region_6.7_spmd.clone.clone, body=%wide.region_4.6_spmd.clone.clone.sunk | while | flops 85656376 | bytes 5683170 | solution.py:82
  170.0 2.5 exponential_select_fusion.2
  172.5 2.8 reshape.363
  175.4 1.1 reduce_max.47
  178.7 2.5 exponential_select_fusion.2
  181.3 2.8 reshape.363
  184.1 1.1 reduce_max.47
  188.1 2.5 exponential_select_fusion.2
  190.6 2.8 reshape.363
  193.5 1.1 reduce_max.47
  197.5 2.5 exponential_select_fusion.2
  200.0 2.8 reshape.363
  202.8 1.1 reduce_max.47
  206.9 2.5 exponential_select_fusion.2
  209.4 2.8 reshape.363
  212.2 1.1 reduce_max.47
  216.2 2.5 exponential_select_fusion.2
  218.8 2.8 reshape.363
  221.6 1.1 reduce_max.47
  225.6 2.5 exponential_select_fusion.2
  228.1 2.8 reshape.363
  231.0 1.1 reduce_max.47
  232.2 0.9 dynamic_update_slice.13
  235.0 2.5 exponential_select_fusion.2
  237.5 2.8 reshape.363
  240.3 1.1 reduce_max.47
  243.6 1.2 fusion.18
  244.8 0.9 convolution_bitcast_fusion
  245.8 311.9 %all-reduce.5.cloned.1.call-done = (f32[128,128]{1,0:T(8,128)}, f32[384,128]{1,0:T(8,128)}) async-done(((f32[128,128]{1,0:T(8,128)}, f32[384,128]{1,0:T(8,128)}), (f32[128,128]{1,0:T(8,128)}, f32[384,128]{1,0:T(8,128)})) %all-reduce.5.cloned.1.call-update) | async-done | bytes 262160 | tf_op jit(solution)/shard_map/psum | solution.py:146
  558.5 207.8 %all-reduce.7.cloned.1.call-done = (f32[128,128]{1,0:T(8,128)}, f32[384,128]{1,0:T(8,128)}) async-done(((f32[128,128]{1,0:T(8,128)}, f32[384,128]{1,0:T(8,128)}), (f32[128,128]{1,0:T(8,128)}, f32[384,128]{1,0:T(8,128)})) %all-reduce.7.cloned.1.call-update) | async-done | bytes 262160 | tf_op jit(solution)/shard_map/psum | solution.py:146
  766.3 1.5 copy.92
  767.7 1.6 copy.93
  (165 shorter events, 38.0 us)
Async XLA Ops:
  7.2 78.0 %copy-start = (f32[384,128]{1,0:T(8,128)S(1)}, f32[384,128]{1,0:T(8,128)}, u32[]{:S(2)}) copy-start(f32[384,128]{1,0:T(8,128)} %param.15) | copy-start | bytes 589828
  7.2 138.9 %all-gather.2.cloned.1.call-start = ((), (), s32[]{:S(2)}) async-start(), calls=%async_computation | async-start | bytes 1081344 | tf_op jit(solution)/shard_map/all_gather | solution.py:111
  7.9 549.8 %all-reduce.5.cloned.1.call-start = ((), (), s32[]{:S(2)}) async-start(), calls=%async_computation.1 | async-start | bytes 524288 | tf_op jit(solution)/shard_map/psum | solution.py:146
  245.8 520.5 %all-reduce.7.cloned.1.call-start = ((), (), s32[]{:S(2)}) async-start(), calls=%async_computation.2 | async-start | bytes 524288 | tf_op jit(solution)/shard_map/psum | solution.py:146
Sparse Core Ops, SparseCore 0:
  10.1 135.9 all-gather.1
  245.9 311.7 all-reduce.4
  560.7 205.5 all-reduce.6
